TPU v7x, 256 devices: a whole 4x4x8 slice. The times are simulated.
256 devices in a mesh: ctx: 32 (over x, z), tp: 8 (over y, core).
Axes of the slice: x: 4, y: 4, z: 8, core: 2. Of those that a mesh axis runs over, the one named last changes fastest.
Arguments:
- hidden_in: bfloat16 [8192, 3072], P('ctx', 'tp'), may hold values from -96 to 96
- norm_gain: float32 [3072], replicated, may hold values from 0.1 to 1.9
- w_query: bfloat16 [3072, 3072], P(None, 'tp'), may hold values from -1 to 1
- w_key: bfloat16 [3072, 3072], P(None, 'tp'), may hold values from -1 to 1
- w_value: bfloat16 [3072, 3072], P(None, 'tp'), may hold values from -0.109375 to 0.109375
- w_out: bfloat16 [3072, 3072], P('tp'), may hold values from -0.109375 to 0.109375
- head_gain: float32 [3072], replicated, may hold values from 0.1 to 1.9
- proj_head: bfloat16 [3072, 2048], P('tp'), may hold values from -0.109375 to 0.109375
- proj_middle: bfloat16 [3072, 512], P('tp'), may hold values from -0.109375 to 0.109375
- proj_tail: bfloat16 [3072, 128], P('tp'), may hold values from -0.109375 to 0.109375
- table_head: bfloat16 [10240, 2048], P(('tp', 'ctx')), may hold values from -64 to 64
- table_middle: bfloat16 [20480, 512], P(('tp', 'ctx')), may hold values from -64 to 64
- table_tail: bfloat16 [104448, 128], P(('tp', 'ctx')), may hold values from -64 to 64
- clusters: bfloat16 [2, 2048], replicated, may hold values from -0.375 to 0.375
- targets: int32 [8192], P('ctx'), may hold values from 0 to 135167
Outputs:
- hidden_out: bfloat16 [8192, 3072], P('ctx', 'tp')
- losses: float32 [8192], P('ctx')
All inputs are finite; a program needn't handle non-finite values.
Results may differ from a plain program's by a relative error of at most 0.004.
Values may be sent and summed in bfloat16 or wider, within the bound.
No kernel may reach another device: no remote copies, remote signals or barrier semaphores. Data moves between devices by JAX's collectives and lax.ppermute only.
A program may use at most 128 MiB of HBM per device.

v0:
```python
import jax
import jax.numpy as jnp
from jax import lax
from jax.sharding import PartitionSpec as P

D = 3072
HD = 96
V0 = 10240
V1 = 20480
NEG_FILL = -1e30


def passed_along(block, axis, distance):
    devices = range(lax.axis_size(axis))
    route = [(i - distance, i) for i in devices if i - distance in devices]
    return lax.ppermute(block, axis, route)


def merged(part, axis, combine):
    gathered = jax.tree.map(lambda a: lax.all_gather(a, axis), part)

    def take(source):
        return jax.tree.map(lambda a: lax.dynamic_index_in_dim(a, source, 0, False), gathered)

    return lax.fori_loop(
        1, lax.axis_size(axis), lambda source, state: combine(state, take(source)), take(0)
    )


def merge_stats(first_stats, second_stats):
    top_value = jnp.maximum(first_stats[0], second_stats[0])
    sum_exp = first_stats[1] * jnp.exp(first_stats[0] - top_value) + second_stats[1] * jnp.exp(
        second_stats[0] - top_value
    )
    return (top_value, sum_exp, first_stats[2] + second_stats[2])


def merge_bands(first_bands, second_bands):
    return tuple(
        (
            merge_stats(one_band, other_band)
            for one_band, other_band in zip(first_bands, second_bands)
        )
    )


def empty_stats(row_total):
    return (
        jnp.full((row_total,), NEG_FILL, jnp.float32),
        jnp.zeros((row_total,), jnp.float32),
        jnp.zeros((row_total,), jnp.float32),
    )


def fold_band(running, table_part, band_rows, local_goal):
    row_count = table_part.shape[0]
    block_rows = min(row_count, 2048)
    for row_start in range(0, row_count, block_rows):
        table_slab = table_part[row_start : row_start + block_rows]
        logits = lax.dot_general(
            table_slab, band_rows, (((1,), (1,)), ((), ())), preferred_element_type=jnp.float32
        )
        word_index = lax.broadcasted_iota(jnp.int32, logits.shape, 0) + row_start
        block_top = jnp.max(logits, 0)
        block_sum = jnp.sum(jnp.exp(logits - block_top[None]), 0)
        block_pick = jnp.sum(jnp.where(word_index == local_goal[None], logits, 0.0), 0)
        running = merge_stats(running, (block_top, block_sum, block_pick))
    return running


def scale_rows(row_values, square_sums, gain_part):
    return (row_values * lax.rsqrt(square_sums / D + 1e-06)[:, None] * gain_part).astype(
        jnp.bfloat16
    )


def project(full_rows, weight):
    return jnp.dot(full_rows, weight, preferred_element_type=jnp.float32).astype(jnp.bfloat16)


def body(
    hidden_in,
    norm_gain,
    w_query,
    w_key,
    w_value,
    w_out,
    head_gain,
    proj_head,
    proj_middle,
    proj_tail,
    table_head,
    table_middle,
    table_tail,
    clusters,
    targets,
):
    seg_len = hidden_in.shape[0]
    local_width = hidden_in.shape[1]
    tp_rank = lax.axis_index("tp")
    ctx_rank = lax.axis_index("ctx")
    ctx_count = lax.axis_size("ctx")
    gain_in = lax.dynamic_slice_in_dim(norm_gain, tp_rank * local_width, local_width)
    gain_out = lax.dynamic_slice_in_dim(head_gain, tp_rank * local_width, local_width)
    own_rows = hidden_in.astype(jnp.float32)
    own_sq = lax.psum(jnp.sum(own_rows * own_rows, 1), "tp")
    own_full = lax.all_gather(scale_rows(own_rows, own_sq, gain_in), "tp", axis=1, tiled=True)
    queries = project(own_full, w_query)
    keys_now = project(own_full, w_key)
    values_now = project(own_full, w_value)
    key_width = keys_now.shape[1]
    carried = passed_along(jnp.concatenate([keys_now, values_now], 1), "ctx", 1)
    memory_keys = carried[:, :key_width]
    memory_values = carried[:, key_width:]
    heads_local = queries.shape[1] // HD
    query_heads = queries.reshape(seg_len, heads_local, HD)
    key_heads = jnp.concatenate([memory_keys, keys_now], 0).reshape(2 * seg_len, heads_local, HD)
    value_heads = jnp.concatenate([memory_values, values_now], 0).reshape(
        2 * seg_len, heads_local, HD
    )
    scores = jnp.einsum(
        "qhe,khe->hqk", query_heads, key_heads, preferred_element_type=jnp.float32
    ) * HD ** (-0.5)
    row_pos = lax.broadcasted_iota(jnp.int32, (seg_len, 2 * seg_len), 0)
    col_pos = lax.broadcasted_iota(jnp.int32, (seg_len, 2 * seg_len), 1)
    allowed = jnp.where(col_pos < seg_len, ctx_rank > 0, col_pos - seg_len <= row_pos)
    scores = jnp.where(allowed[None], scores, NEG_FILL)
    top_score = jnp.max(scores, axis=2, keepdims=True)
    raised = jnp.exp(scores - top_score)
    weights = (raised / jnp.sum(raised, axis=2, keepdims=True)).astype(jnp.bfloat16)
    context = jnp.einsum("hqk,khe->qhe", weights, value_heads, preferred_element_type=jnp.float32)
    context = context.astype(jnp.bfloat16).reshape(seg_len, heads_local * HD)
    partial_out = jnp.dot(context, w_out, preferred_element_type=jnp.float32)
    attention = lax.psum_scatter(
        partial_out.astype(jnp.bfloat16), "tp", scatter_dimension=1, tiled=True
    ).astype(jnp.float32)
    summed = own_rows + attention
    hidden_out = summed.astype(jnp.bfloat16)
    out_sq = lax.psum(jnp.sum(summed * summed, 1), "tp")
    normed_out = scale_rows(summed, out_sq, gain_out)
    band_sums = (
        lax.psum(
            jnp.dot(normed_out, proj_head, preferred_element_type=jnp.float32).astype(jnp.bfloat16),
            "tp",
        ).astype(jnp.float32),
        lax.psum(
            jnp.dot(normed_out, proj_middle, preferred_element_type=jnp.float32).astype(
                jnp.bfloat16
            ),
            "tp",
        ).astype(jnp.float32),
        lax.psum(
            jnp.dot(normed_out, proj_tail, preferred_element_type=jnp.float32).astype(jnp.bfloat16),
            "tp",
        ).astype(jnp.float32),
    )
    inputs_head = band_sums[0].astype(jnp.bfloat16)
    inputs_middle = band_sums[1].astype(jnp.bfloat16)
    inputs_tail = band_sums[2].astype(jnp.bfloat16)
    rows_head = table_head.shape[0]
    rows_middle = table_middle.shape[0]
    rows_tail = table_tail.shape[0]
    head_base = tp_rank * rows_head * ctx_count
    head_stats = fold_band(
        empty_stats(seg_len),
        lax.all_gather(table_head, "ctx", axis=0, tiled=True),
        inputs_head,
        targets - head_base,
    )
    middle_base = tp_rank * rows_middle * ctx_count
    tail_base = tp_rank * rows_tail * ctx_count
    middle_stats = fold_band(
        empty_stats(seg_len),
        lax.all_gather(table_middle, "ctx", axis=0, tiled=True),
        inputs_middle,
        targets - V0 - middle_base,
    )
    tail_stats = fold_band(
        empty_stats(seg_len),
        lax.all_gather(table_tail, "ctx", axis=0, tiled=True),
        inputs_tail,
        targets - V0 - V1 - tail_base,
    )
    head_stats, middle_stats, tail_stats = merged(
        (head_stats, middle_stats, tail_stats), "tp", merge_bands
    )
    word_total = head_stats[0] + jnp.log(head_stats[1])
    cluster_logits = lax.dot_general(
        inputs_head, clusters, (((1,), (1,)), ((), ())), preferred_element_type=jnp.float32
    )
    first_cluster = cluster_logits[:, 0]
    second_cluster = cluster_logits[:, 1]
    highest = jnp.maximum(word_total, jnp.maximum(first_cluster, second_cluster))
    head_total = highest + jnp.log(
        jnp.exp(word_total - highest)
        + jnp.exp(first_cluster - highest)
        + jnp.exp(second_cluster - highest)
    )
    middle_total = middle_stats[0] + jnp.log(middle_stats[1])
    tail_total = tail_stats[0] + jnp.log(tail_stats[1])
    loss_head = head_total - head_stats[2]
    loss_middle = head_total - first_cluster + middle_total - middle_stats[2]
    loss_tail = head_total - second_cluster + tail_total - tail_stats[2]
    losses = jnp.where(
        targets < V0, loss_head, jnp.where(targets < V0 + V1, loss_middle, loss_tail)
    )
    return (hidden_out, losses)


def solution(mesh):
    placed = (
        P("ctx", "tp"),
        P(),
        P(None, "tp"),
        P(None, "tp"),
        P(None, "tp"),
        P("tp", None),
        P(),
        P("tp", None),
        P("tp", None),
        P("tp", None),
        P(("tp", "ctx"), None),
        P(("tp", "ctx"), None),
        P(("tp", "ctx"), None),
        P(),
        P("ctx"),
    )
    return jax.shard_map(
        body, mesh=mesh, in_specs=placed, out_specs=(P("ctx", "tp"), P("ctx")), check_vma=False
    )
```

profile of v0, /device:TPU:1, one launch (start us, length us, event | category | flops | bytes accessed | tf_op | source)
XLA Modules:
  0.0 371.5 jit_solution(5474773820088857261)
XLA Ops:
  9.3 15.0 %psum.35 = f32[256]{0:T(256)S(1)} all-reduce(f32[256]{0:T(256)S(1)} %fusion.52), channel_id=1, replica_groups=mesh['ctx'=32,'tp'=8] {'tp'}, use_global_device_ids=true, to_apply=%region_1.0 | all-reduce | flops 256 | bytes 2048 | tf_op jit(solution)/shard_map/psum | solution.py:106
  26.8 28.5 %all-gather.17.cloned.1.call-done = bf16[256,3072]{1,0:T(8,128)(2,1)} async-done(((bf16[256,384]{1,0:T(8,128)(2,1)}), bf16[256,3072]{1,0:T(8,128)(2,1)}) %all-gather.17.cloned.1.call-update) | async-done | bytes 1572880 | tf_op jit(solution)/shard_map/all_gather | solution.py:107
  55.4 3.3 convolution_convert_fusion.4
  59.7 3.3 collective-permute-start
  67.1 4.0 %collective-permute-done = bf16[256,768]{1,0:T(8,128)(2,1)S(1)} collective-permute-done((bf16[256,768]{1,0:T(8,128)(2,1)S(1)}, bf16[256,768]{1,0:T(8,128)(2,1)S(1)}, u32[]{:S(2)}, u32[]{:S(2)}) %collective-permute-start) | collective-permute-done | bytes 393248 | tf_op jit(solution)/shard_map/ppermute | solution.py:16
  77.9 2.6 copy.26
  82.0 34.9 %reduce-scatter.4.cloned.1.call-done = bf16[384,256]{1,0:T(8,128)(2,1)} async-done(((bf16[3072,256]{1,0:T(8,128)(2,1)}), bf16[384,256]{1,0:T(8,128)(2,1)}) %reduce-scatter.4.cloned.1.call-update) | async-done | bytes 196624
  118.1 14.5 %psum.36 = f32[256]{0:T(256)S(1)} all-reduce(f32[256]{0:T(256)S(1)} %multiply_reduce_fusion), channel_id=1, replica_groups=mesh['ctx'=32,'tp'=8] {'tp'}, use_global_device_ids=true, to_apply=%region_6.7 | all-reduce | flops 256 | bytes 2048 | tf_op jit(solution)/shard_map/psum | solution.py:139
  138.2 22.5 %all-gather.21.cloned.1.call-done = bf16[2560,512]{1,0:T(8,128)(2,1)} async-done(((bf16[80,512]{1,0:T(8,128)(2,1)}), bf16[2560,512]{1,0:T(8,128)(2,1)}) %all-gather.21.cloned.1.call-update) | async-done | bytes 2621456 | tf_op jit(solution)/shard_map/all_gather | solution.py:174
  160.7 43.5 %all-reduce.3.cloned.1.call-done = (bf16[256,2048]{1,0:T(8,128)(2,1)}, bf16[256,512]{1,0:T(8,128)(2,1)}, bf16[256,128]{1,0:T(8,128)(2,1)}) async-done(((bf16[256,2048]{1,0:T(8,128)(2,1)}, bf16[256,512]{1,0:T(8,128)(2,1)}, bf16[256,128]{1,0:T(8,128)(2,1)}), (bf16[256,2048]{1,0:T(8,128)(2,1)}, bf16[256,512]{1,0:T(8,128)(2,1)}, bf16[256,128]{1,0:T(8,128)(2,1)})) %all-reduce.3.cloned.1.call-update) | async-done | bytes 1376272 | tf_op jit(solution)/shard_map/psum | solution.py:142
  206.1 2.5 fusion.72
  209.4 10.6 %all-gather.7 = f32[8,1,256]{2,1,0:T(1,128)S(1)} all-gather(f32[1,1,256]{2,1,0:T(1,128)S(1)} %get-tuple-element.552), channel_id=1, replica_groups=mesh['ctx'=32,'tp'=8] {'tp'}, dimensions={0}, use_global_device_ids=true | all-gather | bytes 9216 | tf_op jit(solution)/shard_map/all_gather | solution.py:20
  220.0 9.4 %all-gather.8 = f32[8,1,256]{2,1,0:T(1,128)S(1)} all-gather(f32[1,1,256]{2,1,0:T(1,128)S(1)} %bitcast.286), channel_id=3, replica_groups=mesh['ctx'=32,'tp'=8] {'tp'}, dimensions={0}, use_global_device_ids=true | all-gather | bytes 9216 | tf_op jit(solution)/shard_map/all_gather | solution.py:20
  229.4 8.4 %all-gather.6 = f32[8,1,256]{2,1,0:T(1,128)S(1)} all-gather(f32[1,1,256]{2,1,0:T(1,128)S(1)} %get-tuple-element.553), channel_id=1, replica_groups=mesh['ctx'=32,'tp'=8] {'tp'}, dimensions={0}, use_global_device_ids=true | all-gather | bytes 9216 | tf_op jit(solution)/shard_map/all_gather | solution.py:20
  237.8 2.7 all-gather.23.cloned.1.call-done
  246.5 3.4 fusion.17
  249.9 15.1 %all-gather.10 = f32[8,1,256]{2,1,0:T(1,128)S(1)} all-gather(f32[1,1,256]{2,1,0:T(1,128)S(1)} %get-tuple-element.548), channel_id=1, replica_groups=mesh['ctx'=32,'tp'=8] {'tp'}, dimensions={0}, use_global_device_ids=true | all-gather | bytes 9216 | tf_op jit(solution)/shard_map/all_gather | solution.py:20
  265.0 8.2 %all-gather.11 = f32[8,1,256]{2,1,0:T(1,128)S(1)} all-gather(f32[1,1,256]{2,1,0:T(1,128)S(1)} %bitcast.287), channel_id=4, replica_groups=mesh['ctx'=32,'tp'=8] {'tp'}, dimensions={0}, use_global_device_ids=true | all-gather | bytes 9216 | tf_op jit(solution)/shard_map/all_gather | solution.py:20
  273.2 9.5 %all-gather.9 = f32[8,1,256]{2,1,0:T(1,128)S(1)} all-gather(f32[1,1,256]{2,1,0:T(1,128)S(1)} %get-tuple-element.549), channel_id=1, replica_groups=mesh['ctx'=32,'tp'=8] {'tp'}, dimensions={0}, use_global_device_ids=true | all-gather | bytes 9216 | tf_op jit(solution)/shard_map/all_gather | solution.py:20
  283.1 42.6 %all-gather.19.cloned.1.call-done = bf16[1280,2048]{1,0:T(8,128)(2,1)} async-done(((bf16[40,2048]{1,0:T(8,128)(2,1)}), bf16[1280,2048]{1,0:T(8,128)(2,1)}) %all-gather.19.cloned.1.call-update) | async-done | bytes 5242896 | tf_op jit(solution)/shard_map/all_gather | solution.py:166
  325.7 4.1 %fusion.70 = (f32[256]{0:T(256)S(1)}, f32[256,1280]{1,0:T(8,128)S(1)}) fusion(bf16[256,2048]{1,0:T(8,128)(2,1)S(1)} %copy-done.5, bf16[1280,2048]{1,0:T(8,128)(2,1)} %all-gather.19.cloned.1.call-done), kind=kOutput, calls=%fused_computation.154 | convolution fusion | flops 1342504704 | bytes 7603200 | tf_op jit(solution)/shard_map/dot_general | solution.py:60
  330.4 14.1 %all-gather.4 = f32[8,1,256]{2,1,0:T(1,128)S(1)} all-gather(f32[1,1,256]{2,1,0:T(1,128)S(1)} %get-tuple-element.557), channel_id=1, replica_groups=mesh['ctx'=32,'tp'=8] {'tp'}, dimensions={0}, use_global_device_ids=true | all-gather | bytes 9216 | tf_op jit(solution)/shard_map/all_gather | solution.py:20
  344.5 8.1 %all-gather.5 = f32[8,1,256]{2,1,0:T(1,128)S(1)} all-gather(f32[1,1,256]{2,1,0:T(1,128)S(1)} %bitcast.281), channel_id=2, replica_groups=mesh['ctx'=32,'tp'=8] {'tp'}, dimensions={0}, use_global_device_ids=true | all-gather | bytes 9216 | tf_op jit(solution)/shard_map/all_gather | solution.py:20
  352.7 9.5 %all-gather.3 = f32[8,1,256]{2,1,0:T(1,128)S(1)} all-gather(f32[1,1,256]{2,1,0:T(1,128)S(1)} %get-tuple-element.558), channel_id=1, replica_groups=mesh['ctx'=32,'tp'=8] {'tp'}, dimensions={0}, use_global_device_ids=true | all-gather | bytes 9216 | tf_op jit(solution)/shard_map/all_gather | solution.py:20
  (197 shorter events, 36.4 us)
Async XLA Ops:
  8.0 67.8 %copy-start = (bf16[384,3072]{1,0:T(8,128)(2,1)S(1)}, bf16[384,3072]{1,0:T(8,128)(2,1)}, u32[]{:S(2)}) copy-start(bf16[384,3072]{1,0:T(8,128)(2,1)} %param.22) | copy-start | bytes 7077892
  8.0 47.3 %all-gather.17.cloned.1.call-start = ((), (), s32[]{:S(2)}) async-start(), calls=%async_computation.1 | async-start | bytes 1769472 | tf_op jit(solution)/shard_map/all_gather | solution.py:107
  26.8 90.1 %reduce-scatter.4.cloned.1.call-start = ((), (), s32[]{:S(2)}) async-start(), calls=%async_computation.5 | async-start | bytes 1769472
  55.4 3.3 copy-start.14
  55.4 3.3 copy-start.16
  58.7 5.1 %copy-start.15 = (bf16[3072,384]{1,0:T(8,128)(2,1)S(1)}, bf16[3072,384]{1,0:T(8,128)(2,1)}, u32[]{:S(2)}) copy-start(bf16[3072,384]{1,0:T(8,128)(2,1)} %param.19) | copy-start | bytes 7077892
  59.7 11.5 %collective-permute-start = (bf16[256,768]{1,0:T(8,128)(2,1)S(1)}, bf16[256,768]{1,0:T(8,128)(2,1)S(1)}, u32[]{:S(2)}, u32[]{:S(2)}) collective-permute-start(bf16[256,768]{1,0:T(8,128)(2,1)S(1)} %pad_maximum_fusion), channel_id=1, source_target_pairs={{0,8},{8,16},{16,24},{24,32},{32,40},{40,48},{48,56},{56,64},{64,7... | collective-permute-start | bytes 1179656 | tf_op jit(solution)/shard_map/ppermute | solution.py:16
  77.9 40.0 %copy-start.3 = (bf16[256,384]{1,0:T(8,128)(2,1)S(1)}, bf16[256,384]{1,0:T(8,128)(2,1)}, u32[]{:S(2)}) copy-start(bf16[256,384]{1,0:T(8,128)(2,1)} %param.17) | copy-start | bytes 589828
  80.5 52.8 %copy-start.8 = (bf16[384,128]{1,0:T(8,128)(2,1)S(1)}, bf16[384,128]{1,0:T(8,128)(2,1)}, u32[]{:S(2)}) copy-start(bf16[384,128]{1,0:T(8,128)(2,1)} %param.26) | copy-start | bytes 294916
  80.5 53.7 %copy-start.6 = (bf16[384,512]{1,0:T(8,128)(2,1)S(1)}, bf16[384,512]{1,0:T(8,128)(2,1)}, u32[]{:S(2)}) copy-start(bf16[384,512]{1,0:T(8,128)(2,1)} %param.25) | copy-start | bytes 1179652
  80.6 80.2 %all-gather.21.cloned.1.call-start = ((), (), s32[]{:S(2)}) async-start(), calls=%async_computation.3 | async-start | bytes 2703360 | tf_op jit(solution)/shard_map/all_gather | solution.py:174
  81.2 123.1 %all-reduce.3.cloned.1.call-start = ((), (), s32[]{:S(2)}) async-start(), calls=%async_computation.6 | async-start | bytes 2752512 | tf_op jit(solution)/shard_map/psum | solution.py:142
  136.9 103.5 %all-gather.23.cloned.1.call-start = ((), (), s32[]{:S(2)}) async-start(), calls=%async_computation.4 | async-start | bytes 3446784 | tf_op jit(solution)/shard_map/all_gather | solution.py:180
  137.5 188.2 %all-gather.19.cloned.1.call-start = ((), (), s32[]{:S(2)}) async-start(), calls=%async_computation.2 | async-start | bytes 5406720 | tf_op jit(solution)/shard_map/all_gather | solution.py:166
  208.6 31.9 %copy-start.2 = (bf16[256,128]{1,0:T(8,128)(2,1)S(1)}, bf16[256,128]{1,0:T(8,128)(2,1)}, u32[]{:S(2)}) copy-start(bf16[256,128]{1,0:T(8,128)(2,1)} %get-tuple-element.529) | copy-start | bytes 196612
  220.0 23.9 %copy-start.10 = (f32[8,1,256]{2,1,0:T(1,128)}, f32[8,1,256]{2,1,0:T(1,128)S(1)}, u32[]{:S(2)}) copy-start(f32[8,1,256]{2,1,0:T(1,128)S(1)} %all-gather.7) | copy-start | bytes 24580
  229.4 14.5 %copy-start.9 = (f32[8,1,256]{2,1,0:T(1,128)}, f32[8,1,256]{2,1,0:T(1,128)S(1)}, u32[]{:S(2)}) copy-start(f32[8,1,256]{2,1,0:T(1,128)S(1)} %all-gather.8) | copy-start | bytes 24580
  237.8 6.1 %copy-start.11 = (f32[8,1,256]{2,1,0:T(1,128)}, f32[8,1,256]{2,1,0:T(1,128)S(1)}, u32[]{:S(2)}) copy-start(f32[8,1,256]{2,1,0:T(1,128)S(1)} %all-gather.6) | copy-start | bytes 24580
  240.5 3.4 copy-start.1
  246.5 36.2 %copy-start.5 = (bf16[256,2048]{1,0:T(8,128)(2,1)S(1)}, bf16[256,2048]{1,0:T(8,128)(2,1)}, u32[]{:S(2)}) copy-start(bf16[256,2048]{1,0:T(8,128)(2,1)} %get-tuple-element.527) | copy-start | bytes 3145732
  246.5 36.2 %copy-start.12 = (bf16[2,2048]{1,0:T(2,128)(2,1)S(1)}, bf16[2,2048]{1,0:T(2,128)(2,1)}, u32[]{:S(2)}) copy-start(bf16[2,2048]{1,0:T(2,128)(2,1)} %param.30) | copy-start | bytes 24580
  283.1 79.1 %slice-start = ((f32[8,1,256]{2,1,0:T(1,128)}), f32[1,1,256]{2,1,0:T(1,128)S(1)}, s32[]{:S(2)}) async-start(f32[8,1,256]{2,1,0:T(1,128)} %copy-done.9), calls=%async_computation.7 | async-start | bytes 2048 | tf_op jit(solution)/shard_map/jit(dynamic_index_in_dim)/dynamic_slice | solution.py:23
  283.1 79.1 %slice-start.1 = ((f32[8,1,256]{2,1,0:T(1,128)}), f32[1,1,256]{2,1,0:T(1,128)S(1)}, s32[]{:S(2)}) async-start(f32[8,1,256]{2,1,0:T(1,128)} %copy-done.10), calls=%async_computation.8 | async-start | bytes 2048 | tf_op jit(solution)/shard_map/jit(dynamic_index_in_dim)/dynamic_slice | solution.py:23
  283.1 79.1 %slice-start.2 = ((f32[8,1,256]{2,1,0:T(1,128)}), f32[1,1,256]{2,1,0:T(1,128)S(1)}, s32[]{:S(2)}) async-start(f32[8,1,256]{2,1,0:T(1,128)} %copy-done.11), calls=%async_computation.9 | async-start | bytes 2048 | tf_op jit(solution)/shard_map/jit(dynamic_index_in_dim)/dynamic_slice | solution.py:23
  (3 other events, 7.5 us)
Sparse Core Ops, SparseCore 0:
  26.9 28.4 all-gather.16
  80.7 36.1 reduce-scatter.3
  137.1 67.1 all-reduce.2
Sparse Core Ops, SparseCore 1:
  83.6 77.0 all-gather.20
  163.2 77.2 all-gather.22
  242.9 82.7 all-gather.18
where the time goes:
time: 372 us
  waiting for transfers between devices  180 us (48%)
  blocking collectives  122 us (33%)
  matrix products  29.8 us (8%)
  between operations  15.8 us (4%)
  other arithmetic  11.3 us (3%)
  local copies, waits for them, and re-layouts  7.9 us (2%)
    all_gather x9, blocking collectives, merged(): gathered = jax.tree.map(lambda a: lax.all_gather(a, axis), part)  92.9 us
    psum x1, waiting for transfers between devices, body(): lax.psum(jnp.dot(normed_out, proj_head, preferred_element_type=jnp.float3...  43.5 us
    all_gather x1, waiting for transfers between devices, body(): lax.all_gather(table_head, 'ctx', axis=0, tiled=True)  42.6 us
    unnamed x7, waiting for transfers between devices  36.5 us
    all_gather x1, waiting for transfers between devices, body(): lax.all_gather(scale_rows(own_rows, own_sq, gain_in), 'tp', axis=1, tiled...  28.5 us
    all_gather x1, waiting for transfers between devices, body(): lax.all_gather(table_middle, 'ctx', axis=0, tiled=True)  22.5 us
    psum x1, blocking collectives, body(): own_sq = lax.psum(jnp.sum(own_rows * own_rows, 1), 'tp')  15 us
    psum x1, blocking collectives, body(): out_sq = lax.psum(jnp.sum(summed * summed, 1), 'tp')  14.5 us
  transfers between devices with their start and end apart: 7, of which 7 were waited for; matrix products, arithmetic and copies ran while one was open for 7% of the time, Pallas kernels for 0%

commit v1 on v0

--- a/solution.py
+++ b/solution.py
@@ -171,7 +171,9 @@
     tail_base = tp_rank * rows_tail * ctx_count
     middle_stats = fold_band(
         empty_stats(seg_len),
-        lax.all_gather(table_middle, "ctx", axis=0, tiled=True),
+        jnp.concatenate(
+            lax.all_to_all(jnp.stack([table_middle] * lax.axis_size("ctx")), "ctx", 0, 0), axis=0
+        ),
         inputs_middle,
         targets - V0 - middle_base,
     )

time: 372 us -> 322 us (0.87)
  waiting for transfers between devices: 180 us -> 124 us
  starting transfers between devices: 3.56 us -> 13.8 us
  blocking collectives: 122 us -> 116 us
    all_gather x1, waiting for transfers between devices: 42.6 us -> 0.03 us  [body(): lax.all_gather(table_head, 'ctx', axis=0, tiled=True)]
    all_gather x1, waiting for transfers between devices: 2.69 us -> 25.7 us  [body(): lax.all_gather(table_tail, 'ctx', axis=0, tiled=True)]
    all_gather x1 -> x0, waiting for transfers between devices: 22.5 us -> none  [body(): lax.all_gather(table_middle, 'ctx', axis=0, tiled=True)]
    psum x1, waiting for transfers between devices: 43.5 us -> 30.1 us  [body(): lax.psum(jnp.dot(normed_out, proj_head, preferred_element_type=jnp.float3...]
    all_to_all x0 -> x1, starting transfers between devices: none -> 10.3 us  [body(): lax.all_to_all(jnp.stack([table_middle] * lax.axis_size('ctx')), 'ctx', 0...]
    all_gather x9, blocking collectives: 92.9 us -> 86.6 us  [merged(): gathered = jax.tree.map(lambda a: lax.all_gather(a, axis), part)]
    unnamed x7 -> x6, waiting for transfers between devices: 36.5 us -> 36 us
  transfers between devices with their start and end apart: 7 -> 7, of which waited for: 7 -> 5; matrix products, arithmetic and copies ran while one was open for 7% -> 8% of each run, Pallas kernels for 0% -> 0%
where the time goes in v1:
time: 322 us; the launch traced here: 321 us
  waiting for transfers between devices  124 us (39%)
  blocking collectives  116 us (36%)
  matrix products  29.7 us (9%)
  between operations  15.6 us (5%)
  starting transfers between devices  13.8 us (4%)
  other arithmetic  11.4 us (4%)
  local copies, waits for them, and re-layouts  9.81 us (3%)
    all_gather x9, blocking collectives, merged(): gathered = jax.tree.map(lambda a: lax.all_gather(a, axis), part)  86.6 us
    unnamed x6, waiting for transfers between devices  36 us
    psum x1, waiting for transfers between devices, body(): lax.psum(jnp.dot(normed_out, proj_head, preferred_element_type=jnp.float3...  30.1 us
    all_gather x1, waiting for transfers between devices, body(): lax.all_gather(scale_rows(own_rows, own_sq, gain_in), 'tp', axis=1, tiled...  28.5 us
    all_gather x1, waiting for transfers between devices, body(): lax.all_gather(table_tail, 'ctx', axis=0, tiled=True)  25.7 us
    psum x1, blocking collectives, body(): own_sq = lax.psum(jnp.sum(own_rows * own_rows, 1), 'tp')  15 us
    psum x1, blocking collectives, body(): out_sq = lax.psum(jnp.sum(summed * summed, 1), 'tp')  14.5 us
    dot_general x10, matrix products, fold_band(): lax.dot_general(table_slab, band_rows, (((1,), (1,)), ((), ())), preferre...  13.7 us
  transfers between devices with their start and end apart: 7, of which 5 were waited for; matrix products, arithmetic and copies ran while one was open for 8% of the time, Pallas kernels for 0%

profile of v1, /device:TPU:1, one launch (start us, length us, event | category | flops | bytes accessed | tf_op | source)
XLA Modules:
  0.0 321.2 jit_solution(7770222255903603815)
XLA Ops:
  9.3 15.0 %psum.35 = f32[256]{0:T(256)S(1)} all-reduce(f32[256]{0:T(256)S(1)} %fusion.52), channel_id=1, replica_groups=mesh['ctx'=32,'tp'=8] {'tp'}, use_global_device_ids=true, to_apply=%region_1.0 | all-reduce | flops 256 | bytes 2048 | tf_op jit(solution)/shard_map/psum | solution.py:106
  26.8 28.5 %all-gather.16.cloned.1.call-done = bf16[256,3072]{1,0:T(8,128)(2,1)} async-done(((bf16[256,384]{1,0:T(8,128)(2,1)}), bf16[256,3072]{1,0:T(8,128)(2,1)}) %all-gather.16.cloned.1.call-update) | async-done | bytes 1572880 | tf_op jit(solution)/shard_map/all_gather | solution.py:107
  55.4 3.3 %convolution_convert_fusion.4 = bf16[256,384]{1,0:T(8,128)(2,1)S(1)} fusion(bf16[256,3072]{1,0:T(8,128)(2,1)} %all-gather.16.cloned.1.call-done, bf16[3072,384]{1,0:T(8,128)(2,1)} %param.21), kind=kOutput, calls=%fused_computation.66 | convolution fusion | flops 604078080 | bytes 4128768 | tf_op jit(solution)/shard_map/dot_general | solution.py:78
  59.7 3.3 %collective-permute-start = (bf16[256,768]{1,0:T(8,128)(2,1)S(1)}, bf16[256,768]{1,0:T(8,128)(2,1)S(1)}, u32[]{:S(2)}, u32[]{:S(2)}) collective-permute-start(bf16[256,768]{1,0:T(8,128)(2,1)S(1)} %pad_maximum_fusion), channel_id=1, source_target_pairs={{0,8},{8,16},{16,24},{24,32},{32,40},{40,48},{48,56},{56,64},{64,7... | collective-permute-start | bytes 1179656 | tf_op jit(solution)/shard_map/ppermute | solution.py:16
  67.1 4.0 %collective-permute-done = bf16[256,768]{1,0:T(8,128)(2,1)S(1)} collective-permute-done((bf16[256,768]{1,0:T(8,128)(2,1)S(1)}, bf16[256,768]{1,0:T(8,128)(2,1)S(1)}, u32[]{:S(2)}, u32[]{:S(2)}) %collective-permute-start) | collective-permute-done | bytes 393248 | tf_op jit(solution)/shard_map/ppermute | solution.py:16
  75.8 2.2 convolution_convert_fusion
  77.9 2.6 copy.26
  82.0 34.9 %reduce-scatter.4.cloned.1.call-done = bf16[384,256]{1,0:T(8,128)(2,1)} async-done(((bf16[3072,256]{1,0:T(8,128)(2,1)}), bf16[384,256]{1,0:T(8,128)(2,1)}) %reduce-scatter.4.cloned.1.call-update) | async-done | bytes 196624
  118.1 14.5 %psum.36 = f32[256]{0:T(256)S(1)} all-reduce(f32[256]{0:T(256)S(1)} %multiply_reduce_fusion), channel_id=1, replica_groups=mesh['ctx'=32,'tp'=8] {'tp'}, use_global_device_ids=true, to_apply=%region_6.7 | all-reduce | flops 256 | bytes 2048 | tf_op jit(solution)/shard_map/psum | solution.py:139
  139.4 10.3 %all-to-all-start = ((bf16[32,80,512]{2,1,0:T(8,128)(2,1)}), bf16[32,80,512]{2,1,0:T(8,128)(2,1)}, u32[]{:S(2)}, u32[]{:S(2)}) async-start(bf16[32,80,512]{2,1,0:T(8,128)(2,1)} %stack.2), calls=%async_computation | async-start | bytes 5242880 | tf_op jit(solution)/shard_map/all_to_all | solution.py:175
  149.8 25.7 %all-gather.20.cloned.1.call-done = bf16[13056,128]{1,0:T(8,128)(2,1)} async-done(((bf16[408,128]{1,0:T(8,128)(2,1)}), bf16[13056,128]{1,0:T(8,128)(2,1)}) %all-gather.20.cloned.1.call-update) | async-done | bytes 3342352 | tf_op jit(solution)/shard_map/all_gather | solution.py:182
  175.6 30.1 %all-reduce.3.cloned.1.call-done = (bf16[256,2048]{1,0:T(8,128)(2,1)}, bf16[256,512]{1,0:T(8,128)(2,1)}, bf16[256,128]{1,0:T(8,128)(2,1)}) async-done(((bf16[256,2048]{1,0:T(8,128)(2,1)}, bf16[256,512]{1,0:T(8,128)(2,1)}, bf16[256,128]{1,0:T(8,128)(2,1)}), (bf16[256,2048]{1,0:T(8,128)(2,1)}, bf16[256,512]{1,0:T(8,128)(2,1)}, bf16[256,128]{1,0:T(8,128)(2,1)})) %all-reduce.3.cloned.1.call-update) | async-done | bytes 1376272 | tf_op jit(solution)/shard_map/psum | solution.py:142
  211.7 3.4 %fusion.17 = (f32[256]{0:T(256)S(1)}, f32[256]{0:T(256)S(1)}, f32[256]{0:T(256)S(1)}, f32[256]{0:T(256)S(1)}, f32[256]{0:T(256)S(1)}, /*index=5*/f32[256]{0:T(25...) fusion(f32[256,2048]{1,0:T(8,128)S(1)} %get-tuple-element.568, ...), kind=kLoop, calls=%fused_computation.41 | loop fusion | flops 15725568 | bytes 12643328 | tf_op jit(solution)/shard_map/reduce_sum | solution.py:66
  215.1 10.6 %all-gather.10 = f32[8,1,256]{2,1,0:T(1,128)S(1)} all-gather(f32[1,1,256]{2,1,0:T(1,128)S(1)} %get-tuple-element.548), channel_id=1, replica_groups=mesh['ctx'=32,'tp'=8] {'tp'}, dimensions={0}, use_global_device_ids=true | all-gather | bytes 9216 | tf_op jit(solution)/shard_map/all_gather | solution.py:20
  225.7 9.4 %all-gather.11 = f32[8,1,256]{2,1,0:T(1,128)S(1)} all-gather(f32[1,1,256]{2,1,0:T(1,128)S(1)} %bitcast.288), channel_id=4, replica_groups=mesh['ctx'=32,'tp'=8] {'tp'}, dimensions={0}, use_global_device_ids=true | all-gather | bytes 9216 | tf_op jit(solution)/shard_map/all_gather | solution.py:20
  235.1 8.2 %all-gather.9 = f32[8,1,256]{2,1,0:T(1,128)S(1)} all-gather(f32[1,1,256]{2,1,0:T(1,128)S(1)} %get-tuple-element.549), channel_id=1, replica_groups=mesh['ctx'=32,'tp'=8] {'tp'}, dimensions={0}, use_global_device_ids=true | all-gather | bytes 9216 | tf_op jit(solution)/shard_map/all_gather | solution.py:20
  245.2 2.4 fusion.72
  248.4 9.5 %all-gather.7 = f32[8,1,256]{2,1,0:T(1,128)S(1)} all-gather(f32[1,1,256]{2,1,0:T(1,128)S(1)} %get-tuple-element.552), channel_id=1, replica_groups=mesh['ctx'=32,'tp'=8] {'tp'}, dimensions={0}, use_global_device_ids=true | all-gather | bytes 9216 | tf_op jit(solution)/shard_map/all_gather | solution.py:20
  257.9 8.2 %all-gather.8 = f32[8,1,256]{2,1,0:T(1,128)S(1)} all-gather(f32[1,1,256]{2,1,0:T(1,128)S(1)} %bitcast.287), channel_id=3, replica_groups=mesh['ctx'=32,'tp'=8] {'tp'}, dimensions={0}, use_global_device_ids=true | all-gather | bytes 9216 | tf_op jit(solution)/shard_map/all_gather | solution.py:20
  266.1 9.5 %all-gather.6 = f32[8,1,256]{2,1,0:T(1,128)S(1)} all-gather(f32[1,1,256]{2,1,0:T(1,128)S(1)} %get-tuple-element.553), channel_id=1, replica_groups=mesh['ctx'=32,'tp'=8] {'tp'}, dimensions={0}, use_global_device_ids=true | all-gather | bytes 9216 | tf_op jit(solution)/shard_map/all_gather | solution.py:20
  276.0 4.1 %fusion.70 = (f32[256]{0:T(256)S(1)}, f32[256,1280]{1,0:T(8,128)S(1)}) fusion(bf16[256,2048]{1,0:T(8,128)(2,1)S(1)} %copy-done.5, bf16[1280,2048]{1,0:T(8,128)(2,1)} %all-gather.18.cloned.1.call-done), kind=kOutput, calls=%fused_computation.154 | convolution fusion | flops 1342504704 | bytes 7603200 | tf_op jit(solution)/shard_map/dot_general | solution.py:60
  280.7 13.7 %all-gather.4 = f32[8,1,256]{2,1,0:T(1,128)S(1)} all-gather(f32[1,1,256]{2,1,0:T(1,128)S(1)} %get-tuple-element.557), channel_id=1, replica_groups=mesh['ctx'=32,'tp'=8] {'tp'}, dimensions={0}, use_global_device_ids=true | all-gather | bytes 9216 | tf_op jit(solution)/shard_map/all_gather | solution.py:20
  294.4 8.1 %all-gather.5 = f32[8,1,256]{2,1,0:T(1,128)S(1)} all-gather(f32[1,1,256]{2,1,0:T(1,128)S(1)} %bitcast.282), channel_id=2, replica_groups=mesh['ctx'=32,'tp'=8] {'tp'}, dimensions={0}, use_global_device_ids=true | all-gather | bytes 9216 | tf_op jit(solution)/shard_map/all_gather | solution.py:20
  302.5 9.5 %all-gather.3 = f32[8,1,256]{2,1,0:T(1,128)S(1)} all-gather(f32[1,1,256]{2,1,0:T(1,128)S(1)} %get-tuple-element.558), channel_id=1, replica_groups=mesh['ctx'=32,'tp'=8] {'tp'}, dimensions={0}, use_global_device_ids=true | all-gather | bytes 9216 | tf_op jit(solution)/shard_map/all_gather | solution.py:20
  (201 shorter events, 35.7 us)
Async XLA Ops:
  8.0 67.8 %copy-start = (bf16[384,3072]{1,0:T(8,128)(2,1)S(1)}, bf16[384,3072]{1,0:T(8,128)(2,1)}, u32[]{:S(2)}) copy-start(bf16[384,3072]{1,0:T(8,128)(2,1)} %param.22) | copy-start | bytes 7077892
  8.0 47.3 %all-gather.16.cloned.1.call-start = ((), (), s32[]{:S(2)}) async-start(), calls=%async_computation.2 | async-start | bytes 1769472 | tf_op jit(solution)/shard_map/all_gather | solution.py:107
  26.8 90.1 %reduce-scatter.4.cloned.1.call-start = ((), (), s32[]{:S(2)}) async-start(), calls=%async_computation.5 | async-start | bytes 1769472
  58.7 5.1 %copy-start.17 = (bf16[3072,384]{1,0:T(8,128)(2,1)S(1)}, bf16[3072,384]{1,0:T(8,128)(2,1)}, u32[]{:S(2)}) copy-start(bf16[3072,384]{1,0:T(8,128)(2,1)} %param.19) | copy-start | bytes 7077892
  59.7 11.5 %collective-permute-start = (bf16[256,768]{1,0:T(8,128)(2,1)S(1)}, bf16[256,768]{1,0:T(8,128)(2,1)S(1)}, u32[]{:S(2)}, u32[]{:S(2)}) collective-permute-start(bf16[256,768]{1,0:T(8,128)(2,1)S(1)} %pad_maximum_fusion), channel_id=1, source_target_pairs={{0,8},{8,16},{16,24},{24,32},{32,40},{40,48},{48,56},{56,64},{64,7... | collective-permute-start | bytes 1179656 | tf_op jit(solution)/shard_map/ppermute | solution.py:16
  77.9 40.0 %copy-start.3 = (bf16[256,384]{1,0:T(8,128)(2,1)S(1)}, bf16[256,384]{1,0:T(8,128)(2,1)}, u32[]{:S(2)}) copy-start(bf16[256,384]{1,0:T(8,128)(2,1)} %param.17) | copy-start | bytes 589828
  80.5 52.8 %copy-start.9 = (bf16[384,128]{1,0:T(8,128)(2,1)S(1)}, bf16[384,128]{1,0:T(8,128)(2,1)}, u32[]{:S(2)}) copy-start(bf16[384,128]{1,0:T(8,128)(2,1)} %param.26) | copy-start | bytes 294916
  80.5 53.6 %copy-start.7 = (bf16[384,512]{1,0:T(8,128)(2,1)S(1)}, bf16[384,512]{1,0:T(8,128)(2,1)}, u32[]{:S(2)}) copy-start(bf16[384,512]{1,0:T(8,128)(2,1)} %param.25) | copy-start | bytes 1179652
  80.6 95.0 %all-gather.20.cloned.1.call-start = ((), (), s32[]{:S(2)}) async-start(), calls=%async_computation.4 | async-start | bytes 3446784 | tf_op jit(solution)/shard_map/all_gather | solution.py:182
  81.2 124.5 %all-reduce.3.cloned.1.call-start = ((), (), s32[]{:S(2)}) async-start(), calls=%async_computation.6 | async-start | bytes 2752512 | tf_op jit(solution)/shard_map/psum | solution.py:142
  136.9 139.1 %all-gather.18.cloned.1.call-start = ((), (), s32[]{:S(2)}) async-start(), calls=%async_computation.3 | async-start | bytes 5406720 | tf_op jit(solution)/shard_map/all_gather | solution.py:166
  139.4 10.4 %copy-start.15 = (s32[256]{0:T(256)S(1)}, s32[256]{0:T(256)}, u32[]{:S(2)}) copy-start(s32[256]{0:T(256)} %param.31) | copy-start | bytes 3076
  139.4 103.9 %all-to-all-start = ((bf16[32,80,512]{2,1,0:T(8,128)(2,1)}), bf16[32,80,512]{2,1,0:T(8,128)(2,1)}, u32[]{:S(2)}, u32[]{:S(2)}) async-start(bf16[32,80,512]{2,1,0:T(8,128)(2,1)} %stack.2), calls=%async_computation | async-start | bytes 5242880 | tf_op jit(solution)/shard_map/all_to_all | solution.py:175
  205.6 3.4 %copy-start.1 = (bf16[13056,128]{1,0:T(8,128)(2,1)S(1)}, bf16[13056,128]{1,0:T(8,128)(2,1)}, u32[]{:S(2)}) copy-start(bf16[13056,128]{1,0:T(8,128)(2,1)} %all-gather.20.cloned.1.call-done) | copy-start | bytes 10027012
  205.6 3.4 %copy-start.2 = (bf16[256,128]{1,0:T(8,128)(2,1)S(1)}, bf16[256,128]{1,0:T(8,128)(2,1)}, u32[]{:S(2)}) copy-start(bf16[256,128]{1,0:T(8,128)(2,1)} %get-tuple-element.529) | copy-start | bytes 196612
  211.7 31.7 %copy-start.6 = (bf16[256,512]{1,0:T(8,128)(2,1)S(1)}, bf16[256,512]{1,0:T(8,128)(2,1)}, u32[]{:S(2)}) copy-start(bf16[256,512]{1,0:T(8,128)(2,1)} %get-tuple-element.528) | copy-start | bytes 786436
  225.7 21.9 %copy-start.12 = (f32[8,1,256]{2,1,0:T(1,128)}, f32[8,1,256]{2,1,0:T(1,128)S(1)}, u32[]{:S(2)}) copy-start(f32[8,1,256]{2,1,0:T(1,128)S(1)} %all-gather.10) | copy-start | bytes 24580
  235.1 12.5 %copy-start.11 = (f32[8,1,256]{2,1,0:T(1,128)}, f32[8,1,256]{2,1,0:T(1,128)S(1)}, u32[]{:S(2)}) copy-start(f32[8,1,256]{2,1,0:T(1,128)S(1)} %all-gather.11) | copy-start | bytes 24580
  243.4 4.3 %copy-start.13 = (f32[8,1,256]{2,1,0:T(1,128)}, f32[8,1,256]{2,1,0:T(1,128)S(1)}, u32[]{:S(2)}) copy-start(f32[8,1,256]{2,1,0:T(1,128)S(1)} %all-gather.9) | copy-start | bytes 24580
  247.6 27.9 %copy-start.5 = (bf16[256,2048]{1,0:T(8,128)(2,1)S(1)}, bf16[256,2048]{1,0:T(8,128)(2,1)}, u32[]{:S(2)}) copy-start(bf16[256,2048]{1,0:T(8,128)(2,1)} %get-tuple-element.527) | copy-start | bytes 3145732
  247.6 27.9 %copy-start.14 = (bf16[2,2048]{1,0:T(2,128)(2,1)S(1)}, bf16[2,2048]{1,0:T(2,128)(2,1)}, u32[]{:S(2)}) copy-start(bf16[2,2048]{1,0:T(2,128)(2,1)} %param.30) | copy-start | bytes 24580
  275.9 36.1 %slice-start = ((f32[8,1,256]{2,1,0:T(1,128)}), f32[1,1,256]{2,1,0:T(1,128)S(1)}, s32[]{:S(2)}) async-start(f32[8,1,256]{2,1,0:T(1,128)} %copy-done.11), calls=%async_computation.7 | async-start | bytes 2048 | tf_op jit(solution)/shard_map/jit(dynamic_index_in_dim)/dynamic_slice | solution.py:23
  275.9 36.1 %slice-start.1 = ((f32[8,1,256]{2,1,0:T(1,128)}), f32[1,1,256]{2,1,0:T(1,128)S(1)}, s32[]{:S(2)}) async-start(f32[8,1,256]{2,1,0:T(1,128)} %copy-done.12), calls=%async_computation.8 | async-start | bytes 2048 | tf_op jit(solution)/shard_map/jit(dynamic_index_in_dim)/dynamic_slice | solution.py:23
  276.0 36.1 %slice-start.2 = ((f32[8,1,256]{2,1,0:T(1,128)}), f32[1,1,256]{2,1,0:T(1,128)S(1)}, s32[]{:S(2)}) async-start(f32[8,1,256]{2,1,0:T(1,128)} %copy-done.13), calls=%async_computation.9 | async-start | bytes 2048 | tf_op jit(solution)/shard_map/jit(dynamic_index_in_dim)/dynamic_slice | solution.py:23
  (5 other events, 13.5 us)
Sparse Core Ops, SparseCore 0:
  26.9 28.4 all-gather.15
  80.7 36.1 reduce-scatter.3
  137.1 68.5 all-reduce.2
Sparse Core Ops, SparseCore 1:
  83.6 91.9 all-gather.19
  178.0 97.5 all-gather.17
